TPU v7x, 32 devices: a whole 2x2x4 slice. The times are simulated.
32 devices in a mesh: member: 2 (over x), tm: 4 (over z), tile: 4 (over y, core).
Axes of the slice: x: 2, y: 2, z: 4, core: 2. Of those that a mesh axis runs over, the one named last changes fastest.
Arguments:
- flux: bfloat16 [64, 32, 16384], P(('member', 'tm'), 'tile'), parts along dimension 0, may hold values from -6 to 6
- footprint: bfloat16 [4, 256, 4, 16384], P('tm', 'tile'), may hold values from 1.4424324e-05 to 0.014404297
- foot_slot: int32 [4, 256, 4], P('tm', 'tile'), may hold values from 0 to 7
- wanted: int32 [4, 4, 4, 2], P('tm', 'tile'), may hold values from 0 to 127
- counts: int32 [4, 4, 4], P('tm', 'tile'), may hold values from 1 to 2
- observed: float32 [4, 256], P('tm', 'tile'), may hold values from -6 to 6
- inv_var: float32 [4, 256], P('tm', 'tile'), may hold values from 25.6 to 102.4
Outputs:
- modeled: float32 [8, 256], P(('member', 'tm'), 'tile'), parts along dimension 0
- gradient: float32 [64, 32, 16384], P(('member', 'tm'), 'tile'), parts along dimension 0
There are 2 independent parts, one for each index of `member`. A program takes and returns all parts, laid end to end along the dimension named above; an argument that names none is the same for every part. Nothing has to cross between parts.
All inputs are finite; a program needn't handle non-finite values.
Results may differ from a plain program's by a relative error of at most 0.0042.
Values may be sent and summed in bfloat16 or wider, within the bound.
No kernel may reach another device: no remote copies, remote signals or barrier semaphores. Data moves between devices by JAX's collectives and lax.ppermute only.
A program may use at most 128 MiB of HBM per device.

v0:
```python
import functools

import jax
import jax.numpy as jnp
from jax import lax
from jax.experimental import pallas as pl
from jax.experimental.pallas import tpu as pltpu
from jax.sharding import PartitionSpec as P


VMEM = pl.BlockSpec(memory_space=pltpu.VMEM)
HBM = pl.BlockSpec(memory_space=pltpu.HBM)
MIB = 1 << 20


def passed_along(value, steps):
    count = lax.axis_size("tm")
    return lax.ppermute(value, "tm", [(source, (source + steps) % count) for source in range(count)])


def swapped(value, mask):
    return lax.ppermute(value, "tile", [(j, j ^ mask) for j in range(lax.axis_size("tile"))])


def in_hbm(value):
    return pltpu.with_memory_space_constraint(value, pltpu.HBM)


def chunks_of(cells, width):
    width = min(width, cells)
    return [(start, width) for start in range(0, cells, width)]


def fetch_kernel(count, start, *refs):
    sources, kept, sems = refs[:count], refs[count : 2 * count], refs[2 * count]
    copies = []
    for n, (source, keep) in enumerate(zip(sources, kept)):
        if source.shape != keep.shape:
            soundings, per, cells = source.shape
            source = source.reshape(soundings * per, cells).at[:, pl.ds(start, keep.shape[1])]
        copies.append(pltpu.make_async_copy(source, keep, sems.at[n]))
        copies[-1].start()
    for copy in copies:
        copy.wait()


def fetched(sources, shapes, start):
    return pl.pallas_call(
        functools.partial(fetch_kernel, len(sources), start),
        in_specs=[HBM] * len(sources),
        out_specs=[VMEM] * len(sources),
        out_shape=[jax.ShapeDtypeStruct(shape, x.dtype) for shape, x in zip(shapes, sources)],
        scratch_shapes=[pltpu.SemaphoreType.DMA((len(sources),))],
        compiler_params=pltpu.CompilerParams(vmem_limit_bytes=12 * MIB),
    )(*[in_hbm(x) for x in sources])


def gather_kernel(owners, capacity, *refs):
    tables, own = refs[:2]
    far, near, now, placing = refs[2], refs[3], refs[4 : 4 + owners], refs[4 + owners]
    own_rows, cells = own.shape
    slots = owners * capacity
    split = owners // 2
    last = lax.axis_index("tm") == lax.axis_size("tm") - 1
    asked = [tables[p, 1] for p in range(owners)] + [tables[p, 0] - own_rows for p in range(owners)]
    asked = jnp.concatenate(asked, axis=0)
    mine = lax.broadcasted_iota(jnp.int32, asked.shape, 1) == lax.axis_index("tile")
    ids = jnp.sum(jnp.where(mine, asked, 0), axis=1, keepdims=True)
    shape = (2 * slots, own_rows)
    ahead = lax.broadcasted_iota(jnp.int32, shape, 0) < jnp.where(last, slots, 0)
    place = one_if((ids == lax.broadcasted_iota(jnp.int32, shape, 1)) & jnp.logical_not(ahead))
    placing[...] = place
    for start, width in chunks_of(cells, cells // 4):
        at = pl.ds(start, width)
        rows = jnp.dot(place, own[:, at], preferred_element_type=jnp.float32).astype(jnp.bfloat16)
        for p in range(owners):
            ahead = rows[p * capacity : (p + 1) * capacity]
            if p < split:
                near[p, :, at] = ahead
            else:
                far[p - split, :, at] = ahead
            now[p][:, at] = rows[slots + p * capacity : slots + (p + 1) * capacity]


def in_parts(value):
    parts, rest = [], value
    for _ in range(3):
        parts.append(rest.astype(jnp.bfloat16).astype(jnp.float32))
        rest = rest - parts[-1]
    return jnp.concatenate(parts + [jnp.zeros((5, value.shape[1]), jnp.float32)], axis=0).astype(jnp.bfloat16)


def spread_by(value, picks, dim):
    parts = lax.dot_general(in_parts(value), picks, (((1,), (dim,)), ((), ())), preferred_element_type=jnp.float32)
    return parts[0:1] + parts[1:2] + parts[2:3]


def one_if(condition):
    return condition.astype(jnp.float32).astype(jnp.bfloat16)


def adjoint_kernel(owners, capacity, per, *refs):
    prints = refs[:2]
    used, counts, observed, inv_var, near, now = refs[2:8]
    arrived = refs[8 : 7 + owners]
    modeled, adjoint = refs[7 + owners], refs[8 + owners : 8 + 2 * owners]
    entries, width = prints[0].shape
    soundings = entries // per
    slots = owners * capacity
    pieces = [(n, start, w) for n in range(len(prints)) for start, w in chunks_of(width, width // 4)]
    shape = (entries, soundings)
    member = one_if(lax.broadcasted_iota(jnp.int32, shape, 0) // per == lax.broadcasted_iota(jnp.int32, shape, 1))
    shape = (entries, entries)
    same = one_if(lax.broadcasted_iota(jnp.int32, shape, 0) // per == lax.broadcasted_iota(jnp.int32, shape, 1) // per)
    measured = spread_by(observed[...], member, 1)
    certain = spread_by(inv_var[...], member, 1)
    entry = jnp.dot(used[...].astype(jnp.float32).astype(jnp.bfloat16), member.T, preferred_element_type=jnp.float32)
    own_entry = lax.broadcasted_iota(jnp.int32, (per, entries), 1) % per == lax.broadcasted_iota(jnp.int32, (per, entries), 0)
    entry = jnp.sum(jnp.where(own_entry, entry, 0.0), axis=0, keepdims=True).astype(jnp.int32)
    slot = lax.broadcasted_iota(jnp.int32, (slots, owners), 0)
    owner, place = (slot // capacity) ^ lax.axis_index("tile"), slot % capacity
    its = owner == lax.broadcasted_iota(jnp.int32, (slots, owners), 1)
    slot_of = jnp.where(its & (place < counts[...]), owner * capacity + place + 1, 0)
    slot_of = jnp.sum(slot_of, axis=1, keepdims=True) - 1
    select = entry == slot_of
    scores = jnp.zeros((slots, entries), jnp.float32)
    for n, start, w in pieces:
        at = pl.ds(n * width + start, w)
        rows = jnp.concatenate([near[0, :, at] + now[:, at]] + [a[:, at] for a in arrived], axis=0)
        part = prints[n][:, pl.ds(start, w)]
        scores += lax.dot_general(rows, part, (((1,), (1,)), ((), ())), preferred_element_type=jnp.float32)
    entry_sums = jnp.sum(jnp.where(select, scores, 0.0), axis=0, keepdims=True)
    coef = ((spread_by(entry_sums, same, 0) - measured) * certain).astype(jnp.bfloat16).astype(jnp.float32)
    spread = jnp.where(select, coef, 0.0).astype(jnp.bfloat16)
    for n, start, w in pieces:
        at = pl.ds(n * width + start, w)
        back = jnp.dot(spread, prints[n][:, pl.ds(start, w)], preferred_element_type=jnp.float32).astype(jnp.bfloat16)
        for p in range(owners):
            adjoint[p][:, at] = back[p * capacity : (p + 1) * capacity]
    modeled[...] = spread_by(entry_sums, member, 0)


def placing_kernel(*refs):
    placing, near, far, returned, (out, held, sems) = refs[0], refs[1], refs[2], refs[3:-3], refs[-3:]
    place = placing[...]
    copies = []
    for n, (start, width) in enumerate(chunks_of(held.shape[1], held.shape[1] // 8)):
        at = pl.ds(start, width)
        rows = [past[p, :, at] for past in (near, far) for p in range(past.shape[0])]
        rows = jnp.concatenate(rows + [r[:, at] for r in returned], axis=0)
        held[:, at] = lax.dot_general(place, rows, (((0,), (0,)), ((), ())), preferred_element_type=jnp.float32)
        copies.append(pltpu.make_async_copy(held.at[:, at], out.at[:, at], sems.at[n]))
        copies[-1].start()
    for copy in copies:
        copy.wait()


def on_device(flux, footprint, foot_slot, wanted, counts, observed, inv_var):
    steps_win, tiles_dev, cells = flux.shape
    owners = lax.axis_size("tile")
    capacity = wanted.shape[3]
    slots = owners * capacity
    own_rows = steps_win * tiles_dev
    soundings, per = foot_slot.shape[1:]
    entries = soundings * per
    half = functools.partial(jax.ShapeDtypeStruct, dtype=jnp.bfloat16)
    params = pltpu.CompilerParams

    table = wanted.reshape(owners, capacity).T
    base = lax.optimization_barrier(jnp.pad(table[None, None], ((0, 0), (0, 1), (0, 0), (0, 0))))
    ahead = passed_along(table, -1)
    tables = base + jnp.pad(ahead[None, None], ((0, 0), (1, 0), (0, 0), (0, 0)))
    while tables.shape[0] < owners:
        theirs = swapped(tables, tables.shape[0])
        tables = jnp.concatenate([tables, theirs])

    prints = footprint.reshape(soundings, per, cells)
    small = [foot_slot.reshape(soundings, per).T, counts.reshape(1, owners), observed, inv_var]
    part = (entries, cells // 2)
    first, *small = fetched([prints] + small, [part] + [x.shape for x in small], 0)
    (second,) = fetched([prints], [part], cells // 2)
    (own,) = fetched([flux.reshape(own_rows, cells)], [(own_rows, cells)], 0)

    block = half((capacity, cells))
    split = owners // 2
    gathered = pl.pallas_call(
        functools.partial(gather_kernel, owners, capacity),
        in_specs=[VMEM, VMEM],
        out_specs=[VMEM] * (owners + 3),
        out_shape=[half((owners - split, capacity, cells)), half((split, capacity, cells))]
        + [block] * owners
        + [half((2 * slots, own_rows))],
        compiler_params=params(vmem_limit_bytes=16 * MIB),
        name="gather",
    )(tables, own)
    far, near, now, placing = gathered[0], gathered[1], gathered[2:-1], gathered[-1]

    far = passed_along(far, 1)
    near = passed_along(near, 1)
    arrived = {}
    for p in [*range(split, owners), *range(1, split)]:
        past = near[p] if p < split else far[p - split]
        arrived[p] = swapped(past + now[p], p)
    arrived = [arrived[p] for p in range(1, owners)]

    results = pl.pallas_call(
        functools.partial(adjoint_kernel, owners, capacity, per),
        in_specs=[VMEM] * (7 + owners),
        out_specs=[VMEM] * (1 + owners),
        out_shape=[jax.ShapeDtypeStruct((1, soundings), jnp.float32)] + [block] * owners,
        compiler_params=params(vmem_limit_bytes=20 * MIB),
        name="adjoint",
    )(
        first,
        second,
        *small,
        near,
        now[0],
        *arrived,
    )
    modeled, adjoint = results[0], results[1:]

    returned = {0: adjoint[0]}
    for p in [*range(split, owners), *range(1, split)]:
        returned[p] = swapped(adjoint[p], p)
    returned = [returned[p] for p in range(owners)]
    near = passed_along(jnp.stack(returned[:split]), -1)
    far = passed_along(jnp.stack(returned[split:]), -1)

    grad = pl.pallas_call(
        placing_kernel,
        in_specs=[VMEM] * (3 + owners),
        out_specs=HBM,
        out_shape=jax.ShapeDtypeStruct((own_rows, cells), jnp.float32),
        scratch_shapes=[pltpu.VMEM((own_rows, cells), jnp.float32), pltpu.SemaphoreType.DMA((8,))],
        compiler_params=params(vmem_limit_bytes=20 * MIB),
        name="placing",
    )(placing, near, far, *returned)
    return (modeled, grad.reshape(steps_win, tiles_dev, cells))


def solution(mesh):
    placed = (
        P(("member", "tm"), "tile", None),
        P("tm", "tile", None, None),
        P("tm", "tile", None),
        P("tm", "tile", None, None),
        P("tm", "tile", None),
        P("tm", "tile"),
        P("tm", "tile"),
    )

    return jax.shard_map(
        on_device,
        mesh=mesh,
        in_specs=placed,
        out_specs=(P(("member", "tm"), "tile"), P(("member", "tm"), "tile", None)),
        check_vma=False,
    )
```

profile of v0, /device:TPU:0, one launch (start us, length us, event | category | flops | bytes accessed | tf_op | source)
XLA Modules:
  0.0 49.3 jit_solution(1203454728400766135)
XLA Ops:
  0.6 5.1 %collective-permute-start = (s32[2,4]{1,0:T(2,128)}, s32[2,4]{1,0:T(2,128)S(1)}, u32[]{:S(2)}, u32[]{:S(2)}) collective-permute-start(s32[2,4]{1,0:T(2,128)} %bitcast.38), channel_id=1, source_target_pairs={{0,12},{4,0},{8,4},{12,8},{1,13},{5,1},{9,5},{13,9},{2,14},{6,2},{... | collective-permute-start | bytes 104 | tf_op jit(solution)/shard_map/ppermute | solution.py:18
  5.8 0.7 %pad.8 = s32[1,2,2,4]{3,2,1,0:T(2,128)S(1)} pad(s32[1,1,2,4]{3,2,1,0:T(2,128)} %bitcast.39, s32[]{:T(128)} %constant.0.clone.1), padding=0_0x0_1x0_0x0_0 | pad | bytes 100 | tf_op jit(solution)/shard_map/jit(_pad)/pad | solution.py:170
  6.5 0.8 %collective-permute-done = s32[2,4]{1,0:T(2,128)S(1)} collective-permute-done((s32[2,4]{1,0:T(2,128)}, s32[2,4]{1,0:T(2,128)S(1)}, u32[]{:S(2)}, u32[]{:S(2)}) %collective-permute-start) | collective-permute-done | bytes 64 | tf_op jit(solution)/shard_map/ppermute | solution.py:18
  7.3 0.0 collective-permute-start.1
  7.3 1.2 %collective-permute-done.1 = s32[1,2,2,4]{3,2,1,0:T(2,128)S(1)} collective-permute-done((s32[1,2,2,4]{3,2,1,0:T(2,128)S(1)}, s32[1,2,2,4]{3,2,1,0:T(2,128)S(1)}, u32[]{:S(2)}, u32[]{:S(2)}) %collective-permute-start.1) | collective-permute-done | bytes 96 | tf_op jit(solution)/shard_map/ppermute | solution.py:22
  8.4 1.5 %collective-permute-start.2 = (s32[2,2,2,4]{3,2,1,0:T(2,128)S(1)}, s32[2,2,2,4]{3,2,1,0:T(2,128)S(1)}, u32[]{:S(2)}, u32[]{:S(2)}) collective-permute-start(s32[2,2,2,4]{3,2,1,0:T(2,128)S(1)} %pad_add_fusion.1), channel_id=1, source_target_pairs={{0,2},{1,3},{2,0},{3,1},{4,6},{5,7},{6,4},{7,5},{8,10},{9,11},{10,... | collective-permute-start | bytes 392 | tf_op jit(solution)/shard_map/ppermute | solution.py:22
  10.0 1.6 %shard_map.88.refs_1_ = bf16[64,16384]{1,0:T(8,128)(2,1)S(1)} custom-call(bf16[64,16384]{1,0:T(8,128)(2,1)} %bitcast.36), custom_call_target="tpu_custom_call" | custom-call | tf_op jit(solution)/shard_map/pallas_call | solution.py:48
  11.6 0.5 collective-permute-done.2
  12.1 0.5 gather.1
  12.6 0.3 collective-permute-start.3
  12.9 1.6 %collective-permute-start.5 = (bf16[2,2,16384]{2,1,0:T(2,128)(2,1)S(1)}, bf16[2,2,16384]{2,1,0:T(2,128)(2,1)S(1)}, u32[]{:S(2)}, u32[]{:S(2)}) collective-permute-start(bf16[2,2,16384]{2,1,0:T(2,128)(2,1)S(1)} %get-tuple-element.27), channel_id=1, source_target_pairs={{0,4},{4,8},{8,12},{12,0},{1,5},{5,9},{9,13},{13,1},{2,6},{6,10},{... | collective-permute-start | bytes 393224 | tf_op jit(solution)/shard_map/ppermute | solution.py:18
  14.4 6.6 %collective-permute-done.3.refs_6_ = bf16[2,2,16384]{2,1,0:T(2,128)(2,1)S(1)} collective-permute-done((bf16[2,2,16384]{2,1,0:T(2,128)(2,1)S(1)}, bf16[2,2,16384]{2,1,0:T(2,128)(2,1)S(1)}, u32[]{:S(2)}, u32[]{:S(2)}) %collective-permute-start.3) | collective-permute-done | bytes 131104 | tf_op jit(solution)/shard_map/ppermute | solution.py:18
  21.0 0.1 fusion.2
  21.1 0.1 collective-permute-start.4
  21.2 1.4 %collective-permute-done.5 = bf16[2,2,16384]{2,1,0:T(2,128)(2,1)S(1)} collective-permute-done((bf16[2,2,16384]{2,1,0:T(2,128)(2,1)S(1)}, bf16[2,2,16384]{2,1,0:T(2,128)(2,1)S(1)}, u32[]{:S(2)}, u32[]{:S(2)}) %collective-permute-start.5) | collective-permute-done | bytes 131104 | tf_op jit(solution)/shard_map/ppermute | solution.py:18
  22.6 0.1 fusion
  22.7 0.1 collective-permute-start.7
  22.8 1.2 %collective-permute-start.6 = (bf16[2,16384]{1,0:T(2,128)(2,1)S(1)}, bf16[2,16384]{1,0:T(2,128)(2,1)S(1)}, u32[]{:S(2)}, u32[]{:S(2)}) collective-permute-start(bf16[2,16384]{1,0:T(2,128)(2,1)S(1)} %get-tuple-element.37), channel_id=1, source_target_pairs={{0,2},{1,3},{2,0},{3,1},{4,6},{5,7},{6,4},{7,5},{8,10},{9,11},{10,... | collective-permute-start | bytes 196616 | tf_op jit(solution)/shard_map/ppermute | solution.py:22
  24.0 2.2 %shard_map.87.refs_1_ = bf16[256,8192]{1,0:T(8,128)(2,1)S(1)} custom-call(bf16[64,4,16384]{2,1,0:T(4,128)(2,1)} %bitcast.33), custom_call_target="tpu_custom_call" | custom-call | tf_op jit(solution)/shard_map/pallas_call | solution.py:48
  26.2 2.3 %shard_map.86 = (bf16[256,8192]{1,0:T(8,128)(2,1)S(1)}, s32[4,64]{1,0:T(4,128)S(1)}, s32[1,4]{1,0:T(1,128)S(1)}, f32[1,64]{1,0:T(1,128)S(1)}, f32[1,64]{1,0:T(1,128)S(1)}) custom-call(bf16[64,4,16384]{2,1,0:T(4,128)(2,1)} %bitcast.34, s32[4,64]{1,0:T(4,128)} %bitcast.37, s32[1,4]{1,0:T(1,128)} %bitcast.41, f32[1,64]{1,0:T(1,128)} %refs_3_.1, f32[1,64]{1,0:T(1,128)} %refs_4_.1), custom_call_target="tpu_custom_call" | custom-call | tf_op jit(solution)/shard_map/pallas_call | solution.py:48
  28.5 0.0 collective-permute-done.4.refs_8_
  28.5 0.0 collective-permute-done.7.refs_10_
  28.5 0.0 collective-permute-done.6.refs_9_
  28.5 6.4 %adjoint.1 = (f32[1,64]{1,0:T(1,128)}, bf16[2,16384]{1,0:T(2,128)(2,1)S(1)}, bf16[2,16384]{1,0:T(2,128)(2,1)S(1)}, bf16[2,16384]{1,0:T(2,128)(2,1)S(1)}, bf16[2,16384]{1,0:T(2,128)(2,1)S(1)}) custom-call(bf16[256,8192]{1,0:T(8,128)(2,1)S(1)} %get-tuple-element.19.refs_0_, bf16[256,8192]{1,0:T(8,128)(2,1)S(1)} %shard_map.87.refs_1_, ...), custom_call_target="tpu_custom_call" | custom-call | tf_op jit(solution)/shard_map/adjoint/pallas_call | solution.py:206
  34.9 0.7 %collective-permute-start.8 = (bf16[2,16384]{1,0:T(2,128)(2,1)S(1)}, bf16[2,16384]{1,0:T(2,128)(2,1)S(1)}, u32[]{:S(2)}, u32[]{:S(2)}) collective-permute-start(bf16[2,16384]{1,0:T(2,128)(2,1)S(1)} %get-tuple-element.33), channel_id=1, source_target_pairs={{0,1},{1,0},{2,3},{3,2},{4,5},{5,4},{6,7},{7,6},{8,9},{9,8},{10,11... | collective-permute-start | bytes 196616 | tf_op jit(solution)/shard_map/ppermute | solution.py:22
  35.6 1.1 %collective-permute-start.10 = (bf16[2,16384]{1,0:T(2,128)(2,1)S(1)}, bf16[2,16384]{1,0:T(2,128)(2,1)S(1)}, u32[]{:S(2)}, u32[]{:S(2)}) collective-permute-start(bf16[2,16384]{1,0:T(2,128)(2,1)S(1)} %get-tuple-element.34), channel_id=1, source_target_pairs={{0,2},{1,3},{2,0},{3,1},{4,6},{5,7},{6,4},{7,5},{8,10},{9,11},{10,... | collective-permute-start | bytes 196616 | tf_op jit(solution)/shard_map/ppermute | solution.py:22
  36.7 0.2 collective-permute-start.11
  36.9 0.0 collective-permute-done.8.refs_4_
  36.9 0.2 pad_maximum_fusion
  37.1 1.8 %collective-permute-start.9 = (bf16[2,2,16384]{2,1,0:T(2,128)(2,1)S(1)}, bf16[2,2,16384]{2,1,0:T(2,128)(2,1)S(1)}, u32[]{:S(2)}, u32[]{:S(2)}) collective-permute-start(bf16[2,2,16384]{2,1,0:T(2,128)(2,1)S(1)} %pad_maximum_fusion), channel_id=1, source_target_pairs={{0,12},{4,0},{8,4},{12,8},{1,13},{5,1},{9,5},{13,9},{2,14},{6,2},{... | collective-permute-start | bytes 393224 | tf_op jit(solution)/shard_map/ppermute | solution.py:18
  38.9 1.1 %collective-permute-done.10.refs_5_ = bf16[2,16384]{1,0:T(2,128)(2,1)S(1)} collective-permute-done((bf16[2,16384]{1,0:T(2,128)(2,1)S(1)}, bf16[2,16384]{1,0:T(2,128)(2,1)S(1)}, u32[]{:S(2)}, u32[]{:S(2)}) %collective-permute-start.10) | collective-permute-done | bytes 65568 | tf_op jit(solution)/shard_map/ppermute | solution.py:22
  40.0 1.1 %collective-permute-done.11.refs_6_ = bf16[2,16384]{1,0:T(2,128)(2,1)S(1)} collective-permute-done((bf16[2,16384]{1,0:T(2,128)(2,1)S(1)}, bf16[2,16384]{1,0:T(2,128)(2,1)S(1)}, u32[]{:S(2)}, u32[]{:S(2)}) %collective-permute-start.11) | collective-permute-done | bytes 65568 | tf_op jit(solution)/shard_map/ppermute | solution.py:22
  41.1 0.2 pad_maximum_fusion.1
  41.2 1.8 %collective-permute-start.12 = (bf16[2,2,16384]{2,1,0:T(2,128)(2,1)S(1)}, bf16[2,2,16384]{2,1,0:T(2,128)(2,1)S(1)}, u32[]{:S(2)}, u32[]{:S(2)}) collective-permute-start(bf16[2,2,16384]{2,1,0:T(2,128)(2,1)S(1)} %pad_maximum_fusion.1), channel_id=1, source_target_pairs={{0,12},{4,0},{8,4},{12,8},{1,13},{5,1},{9,5},{13,9},{2,14},{6,2},{... | collective-permute-start | bytes 393224 | tf_op jit(solution)/shard_map/ppermute | solution.py:18
  43.0 0.3 collective-permute-done.9.refs_1_
  43.3 3.6 %collective-permute-done.12.refs_2_ = bf16[2,2,16384]{2,1,0:T(2,128)(2,1)S(1)} collective-permute-done((bf16[2,2,16384]{2,1,0:T(2,128)(2,1)S(1)}, bf16[2,2,16384]{2,1,0:T(2,128)(2,1)S(1)}, u32[]{:S(2)}, u32[]{:S(2)}) %collective-permute-start.12) | collective-permute-done | bytes 131104 | tf_op jit(solution)/shard_map/ppermute | solution.py:18
  47.0 2.3 %placing.1 = f32[64,16384]{1,0:T(8,128)} custom-call(bf16[16,64]{1,0:T(8,128)(2,1)S(1)} %get-tuple-element.31.refs_0_, bf16[2,2,16384]{2,1,0:T(2,128)(2,1)S(1)} %collective-permute-done.9.refs_1_, bf16[2,2,16384]{2,1,0:T(2,128)(2,1)S(1)} %collective-permute-done.12.refs_2_, bf16[2,16384]{1,0:T(2,128)(2,1)S(1)} %get-tuple-element.32.refs_3_, ...), custom_call_target="tpu_custom_call" | custom-call | tf_op jit(solution)/shard_map/placing/pallas_call | solution.py:230
  (3 shorter events, 0.0 us)
Async XLA Ops:
  0.6 6.6 %collective-permute-start = (s32[2,4]{1,0:T(2,128)}, s32[2,4]{1,0:T(2,128)S(1)}, u32[]{:S(2)}, u32[]{:S(2)}) collective-permute-start(s32[2,4]{1,0:T(2,128)} %bitcast.38), channel_id=1, source_target_pairs={{0,12},{4,0},{8,4},{12,8},{1,13},{5,1},{9,5},{13,9},{2,14},{6,2},{... | collective-permute-start | bytes 104 | tf_op jit(solution)/shard_map/ppermute | solution.py:18
  7.3 1.2 %collective-permute-start.1 = (s32[1,2,2,4]{3,2,1,0:T(2,128)S(1)}, s32[1,2,2,4]{3,2,1,0:T(2,128)S(1)}, u32[]{:S(2)}, u32[]{:S(2)}) collective-permute-start(s32[1,2,2,4]{3,2,1,0:T(2,128)S(1)} %pad_add_fusion.2), channel_id=1, source_target_pairs={{0,1},{1,0},{2,3},{3,2},{4,5},{5,4},{6,7},{7,6},{8,9},{9,8},{10,11... | collective-permute-start | bytes 200 | tf_op jit(solution)/shard_map/ppermute | solution.py:22
  8.4 3.6 %collective-permute-start.2 = (s32[2,2,2,4]{3,2,1,0:T(2,128)S(1)}, s32[2,2,2,4]{3,2,1,0:T(2,128)S(1)}, u32[]{:S(2)}, u32[]{:S(2)}) collective-permute-start(s32[2,2,2,4]{3,2,1,0:T(2,128)S(1)} %pad_add_fusion.1), channel_id=1, source_target_pairs={{0,2},{1,3},{2,0},{3,1},{4,6},{5,7},{6,4},{7,5},{8,10},{9,11},{10,... | collective-permute-start | bytes 392 | tf_op jit(solution)/shard_map/ppermute | solution.py:22
  12.6 8.5 %collective-permute-start.3 = (bf16[2,2,16384]{2,1,0:T(2,128)(2,1)S(1)}, bf16[2,2,16384]{2,1,0:T(2,128)(2,1)S(1)}, u32[]{:S(2)}, u32[]{:S(2)}) collective-permute-start(bf16[2,2,16384]{2,1,0:T(2,128)(2,1)S(1)} %get-tuple-element.24), channel_id=1, source_target_pairs={{0,4},{4,8},{8,12},{12,0},{1,5},{5,9},{9,13},{13,1},{2,6},{6,10},{... | collective-permute-start | bytes 393224 | tf_op jit(solution)/shard_map/ppermute | solution.py:18
  12.9 9.7 %collective-permute-start.5 = (bf16[2,2,16384]{2,1,0:T(2,128)(2,1)S(1)}, bf16[2,2,16384]{2,1,0:T(2,128)(2,1)S(1)}, u32[]{:S(2)}, u32[]{:S(2)}) collective-permute-start(bf16[2,2,16384]{2,1,0:T(2,128)(2,1)S(1)} %get-tuple-element.27), channel_id=1, source_target_pairs={{0,4},{4,8},{8,12},{12,0},{1,5},{5,9},{9,13},{13,1},{2,6},{6,10},{... | collective-permute-start | bytes 393224 | tf_op jit(solution)/shard_map/ppermute | solution.py:18
  21.1 7.4 %collective-permute-start.4 = (bf16[2,16384]{1,0:T(2,128)(2,1)S(1)}, bf16[2,16384]{1,0:T(2,128)(2,1)S(1)}, u32[]{:S(2)}, u32[]{:S(2)}) collective-permute-start(bf16[2,16384]{1,0:T(2,128)(2,1)S(1)} %fusion.2), channel_id=1, source_target_pairs={{0,1},{1,0},{2,3},{3,2},{4,5},{5,4},{6,7},{7,6},{8,9},{9,8},{10,11... | collective-permute-start | bytes 196616 | tf_op jit(solution)/shard_map/ppermute | solution.py:22
  22.7 5.8 %collective-permute-start.7 = (bf16[2,16384]{1,0:T(2,128)(2,1)S(1)}, bf16[2,16384]{1,0:T(2,128)(2,1)S(1)}, u32[]{:S(2)}, u32[]{:S(2)}) collective-permute-start(bf16[2,16384]{1,0:T(2,128)(2,1)S(1)} %get-tuple-element.36), channel_id=1, source_target_pairs={{0,3},{1,2},{2,1},{3,0},{4,7},{5,6},{6,5},{7,4},{8,11},{9,10},{10,... | collective-permute-start | bytes 196616 | tf_op jit(solution)/shard_map/ppermute | solution.py:22
  22.8 5.7 %collective-permute-start.6 = (bf16[2,16384]{1,0:T(2,128)(2,1)S(1)}, bf16[2,16384]{1,0:T(2,128)(2,1)S(1)}, u32[]{:S(2)}, u32[]{:S(2)}) collective-permute-start(bf16[2,16384]{1,0:T(2,128)(2,1)S(1)} %get-tuple-element.37), channel_id=1, source_target_pairs={{0,2},{1,3},{2,0},{3,1},{4,6},{5,7},{6,4},{7,5},{8,10},{9,11},{10,... | collective-permute-start | bytes 196616 | tf_op jit(solution)/shard_map/ppermute | solution.py:22
  34.9 2.0 %collective-permute-start.8 = (bf16[2,16384]{1,0:T(2,128)(2,1)S(1)}, bf16[2,16384]{1,0:T(2,128)(2,1)S(1)}, u32[]{:S(2)}, u32[]{:S(2)}) collective-permute-start(bf16[2,16384]{1,0:T(2,128)(2,1)S(1)} %get-tuple-element.33), channel_id=1, source_target_pairs={{0,1},{1,0},{2,3},{3,2},{4,5},{5,4},{6,7},{7,6},{8,9},{9,8},{10,11... | collective-permute-start | bytes 196616 | tf_op jit(solution)/shard_map/ppermute | solution.py:22
  35.6 4.4 %collective-permute-start.10 = (bf16[2,16384]{1,0:T(2,128)(2,1)S(1)}, bf16[2,16384]{1,0:T(2,128)(2,1)S(1)}, u32[]{:S(2)}, u32[]{:S(2)}) collective-permute-start(bf16[2,16384]{1,0:T(2,128)(2,1)S(1)} %get-tuple-element.34), channel_id=1, source_target_pairs={{0,2},{1,3},{2,0},{3,1},{4,6},{5,7},{6,4},{7,5},{8,10},{9,11},{10,... | collective-permute-start | bytes 196616 | tf_op jit(solution)/shard_map/ppermute | solution.py:22
  36.7 4.4 %collective-permute-start.11 = (bf16[2,16384]{1,0:T(2,128)(2,1)S(1)}, bf16[2,16384]{1,0:T(2,128)(2,1)S(1)}, u32[]{:S(2)}, u32[]{:S(2)}) collective-permute-start(bf16[2,16384]{1,0:T(2,128)(2,1)S(1)} %get-tuple-element.35), channel_id=1, source_target_pairs={{0,3},{1,2},{2,1},{3,0},{4,7},{5,6},{6,5},{7,4},{8,11},{9,10},{10,... | collective-permute-start | bytes 196616 | tf_op jit(solution)/shard_map/ppermute | solution.py:22
  37.1 6.2 %collective-permute-start.9 = (bf16[2,2,16384]{2,1,0:T(2,128)(2,1)S(1)}, bf16[2,2,16384]{2,1,0:T(2,128)(2,1)S(1)}, u32[]{:S(2)}, u32[]{:S(2)}) collective-permute-start(bf16[2,2,16384]{2,1,0:T(2,128)(2,1)S(1)} %pad_maximum_fusion), channel_id=1, source_target_pairs={{0,12},{4,0},{8,4},{12,8},{1,13},{5,1},{9,5},{13,9},{2,14},{6,2},{... | collective-permute-start | bytes 393224 | tf_op jit(solution)/shard_map/ppermute | solution.py:18
  41.2 5.7 %collective-permute-start.12 = (bf16[2,2,16384]{2,1,0:T(2,128)(2,1)S(1)}, bf16[2,2,16384]{2,1,0:T(2,128)(2,1)S(1)}, u32[]{:S(2)}, u32[]{:S(2)}) collective-permute-start(bf16[2,2,16384]{2,1,0:T(2,128)(2,1)S(1)} %pad_maximum_fusion.1), channel_id=1, source_target_pairs={{0,12},{4,0},{8,4},{12,8},{1,13},{5,1},{9,5},{13,9},{2,14},{6,2},{... | collective-permute-start | bytes 393224 | tf_op jit(solution)/shard_map/ppermute | solution.py:18
where the time goes:
time: 49.5 us; the launch traced here: 49.3 us
  waiting for transfers between devices  16.5 us (33%)
  starting transfers between devices  15.5 us (31%)
  Pallas kernels  15.3 us (31%)
  between operations  0.73 us (1%)
  local copies, waits for them, and re-layouts  0.72 us (1%)
  other arithmetic  0.59 us (1%)
    ppermute x5, waiting for transfers between devices, passed_along(): lax.ppermute(value, 'tm', [(source, (source + steps) % count) for source...  12.7 us
    ppermute x5, starting transfers between devices, passed_along(): lax.ppermute(value, 'tm', [(source, (source + steps) % count) for source...  10.6 us
    pallas_call x1, Pallas kernels, on_device(): pl.pallas_call(functools.partial(adjoint_kernel, owners, capacity, per),...  6.35 us
    pallas_call x3, Pallas kernels, fetched(): pl.pallas_call(functools.partial(fetch_kernel, len(sources), start), in_s...  6.11 us
    ppermute x8, starting transfers between devices, swapped(): lax.ppermute(value, 'tile', [(j, j ^ mask) for j in range(lax.axis_size('...  4.87 us
    ppermute x8, waiting for transfers between devices, swapped(): lax.ppermute(value, 'tile', [(j, j ^ mask) for j in range(lax.axis_size('...  3.82 us
    pallas_call x1, Pallas kernels, on_device(): pl.pallas_call(placing_kernel, in_specs=[VMEM] * (3 + owners), out_specs=...  2.33 us
  transfers between devices with their start and end apart: 13, of which 9 were waited for; matrix products, arithmetic and copies ran while one was open for 3% of the time, Pallas kernels for 12%

commit v1 on v0

v1 whole, which is shorter than its diff:
```python
import functools

import jax
import jax.numpy as jnp
from jax import lax
from jax.experimental import pallas as pl
from jax.experimental.pallas import tpu as pltpu
from jax.sharding import PartitionSpec as P


VMEM = pl.BlockSpec(memory_space=pltpu.VMEM)
HBM = pl.BlockSpec(memory_space=pltpu.HBM)
MIB = 1 << 20
PARTS = (1, 3, 4)


def passed_along(value, steps, ring):
    count = lax.axis_size("tm")
    sources = range(count) if ring else range(max(0, -steps), min(count, count - steps))
    return lax.ppermute(value, "tm", [(source, (source + steps) % count) for source in sources])


def swapped(value, mask):
    return lax.ppermute(value, "tile", [(j, j ^ mask) for j in range(lax.axis_size("tile"))])


def in_hbm(value):
    return pltpu.with_memory_space_constraint(value, pltpu.HBM)


def chunks_of(cells, width):
    width = min(width, cells)
    return [(start, width) for start in range(0, cells, width)]


def fetch_kernel(count, start, *refs):
    sources, kept, sems = refs[:count], refs[count : 2 * count], refs[2 * count]
    copies = []
    for n, (source, keep) in enumerate(zip(sources, kept)):
        if len(source.shape) == 3:
            soundings, per, cells = source.shape
            source = source.reshape(soundings * per, cells).at[:, pl.ds(start, keep.shape[1])]
        width = keep.shape[1]
        for m, (at, w) in enumerate(chunks_of(width, width // 4 if width % 4096 == 0 else width)):
            piece = pltpu.make_async_copy(source.at[:, pl.ds(at, w)], keep.at[:, pl.ds(at, w)], sems.at[n, m])
            piece.start()
            copies.append(piece)
    for copy in copies:
        copy.wait()


def fetched(sources, shapes, start):
    return pl.pallas_call(
        functools.partial(fetch_kernel, len(sources), start),
        in_specs=[HBM] * len(sources),
        out_specs=[VMEM] * len(sources),
        out_shape=[jax.ShapeDtypeStruct(shape, x.dtype) for shape, x in zip(shapes, sources)],
        scratch_shapes=[pltpu.SemaphoreType.DMA((len(sources), 4))],
        compiler_params=pltpu.CompilerParams(vmem_limit_bytes=12 * MIB),
    )(*[in_hbm(x) for x in sources])


def gather_kernel(owners, capacity, *refs):
    tables, own = refs[:2]
    later, now, placing = refs[2 : 2 + owners], refs[2 + owners : 2 + 2 * owners], refs[2 + 2 * owners]
    own_rows, cells = own.shape
    slots = owners * capacity
    last = lax.axis_index("tm") == lax.axis_size("tm") - 1
    asked = [tables[p, 1] for p in range(owners)] + [tables[p, 0] - own_rows for p in range(owners)]
    asked = jnp.concatenate(asked, axis=0)
    mine = lax.broadcasted_iota(jnp.int32, asked.shape, 1) == lax.axis_index("tile")
    ids = jnp.sum(jnp.where(mine, asked, 0), axis=1, keepdims=True)
    shape = (2 * slots, own_rows)
    ahead = lax.broadcasted_iota(jnp.int32, shape, 0) < jnp.where(last, slots, 0)
    place = one_if((ids == lax.broadcasted_iota(jnp.int32, shape, 1)) & jnp.logical_not(ahead))
    placing[...] = place
    for start, width in chunks_of(cells, cells // 4):
        at = pl.ds(start, width)
        rows = jnp.dot(place, own[:, at], preferred_element_type=jnp.float32).astype(jnp.bfloat16)
        for p in range(owners):
            later[p][:, at] = rows[p * capacity : (p + 1) * capacity]
            now[p][:, at] = rows[slots + p * capacity : slots + (p + 1) * capacity]


def in_parts(value):
    parts, rest = [], value
    for _ in range(3):
        parts.append(rest.astype(jnp.bfloat16).astype(jnp.float32))
        rest = rest - parts[-1]
    return jnp.concatenate(parts + [jnp.zeros((5, value.shape[1]), jnp.float32)], axis=0).astype(jnp.bfloat16)


def spread_by(value, picks, dim):
    parts = lax.dot_general(in_parts(value), picks, (((1,), (dim,)), ((), ())), preferred_element_type=jnp.float32)
    return parts[0:1] + parts[1:2] + parts[2:3]


def one_if(condition):
    return condition.astype(jnp.float32).astype(jnp.bfloat16)


def adjoint_kernel(owners, capacity, per, *refs):
    used, counts, observed, inv_var, past, now = refs[3:9]
    arrived = refs[9 : 8 + owners]
    modeled, adjoint = refs[8 + owners], refs[9 + owners : 9 + 2 * owners]
    third, sems = refs[9 + 2 * owners :]
    prints = refs[:2] + (third,)
    entries, cells = prints[0].shape[0], past.shape[1]
    unit = cells // 8
    rest = refs[2].reshape(entries, cells)
    copies = []
    for n, (start, w) in enumerate(chunks_of(third.shape[1], unit)):
        source = rest.at[:, pl.ds(cells - third.shape[1] + start, w)]
        copies.append(pltpu.make_async_copy(source, third.at[:, pl.ds(start, w)], sems.at[n]))
        copies[-1].start()
    soundings = entries // per
    slots = owners * capacity
    pieces = [(part, start, w) for part in prints for start, w in chunks_of(part.shape[1], unit)]
    shape = (entries, soundings)
    member = one_if(lax.broadcasted_iota(jnp.int32, shape, 0) // per == lax.broadcasted_iota(jnp.int32, shape, 1))
    shape = (entries, entries)
    same = one_if(lax.broadcasted_iota(jnp.int32, shape, 0) // per == lax.broadcasted_iota(jnp.int32, shape, 1) // per)
    measured = spread_by(observed[...], member, 1)
    certain = spread_by(inv_var[...], member, 1)
    entry = jnp.dot(used[...].astype(jnp.float32).astype(jnp.bfloat16), member.T, preferred_element_type=jnp.float32)
    own_entry = lax.broadcasted_iota(jnp.int32, (per, entries), 1) % per == lax.broadcasted_iota(jnp.int32, (per, entries), 0)
    entry = jnp.sum(jnp.where(own_entry, entry, 0.0), axis=0, keepdims=True).astype(jnp.int32)
    slot = lax.broadcasted_iota(jnp.int32, (slots, owners), 0)
    owner, place = (slot // capacity) ^ lax.axis_index("tile"), slot % capacity
    its = owner == lax.broadcasted_iota(jnp.int32, (slots, owners), 1)
    slot_of = jnp.where(its & (place < counts[...]), owner * capacity + place + 1, 0)
    slot_of = jnp.sum(slot_of, axis=1, keepdims=True) - 1
    select = entry == slot_of
    scores = jnp.zeros((slots, entries), jnp.float32)
    for n, (part, start, w) in enumerate(pieces):
        at = pl.ds(n * unit, unit)
        rows = jnp.concatenate([past[:, at] + now[:, at]] + [a[:, at] for a in arrived], axis=0)
        if part is third:
            copies[start // unit].wait()
        scores += lax.dot_general(rows, part[:, pl.ds(start, w)], (((1,), (1,)), ((), ())), preferred_element_type=jnp.float32)
    entry_sums = jnp.sum(jnp.where(select, scores, 0.0), axis=0, keepdims=True)
    coef = ((spread_by(entry_sums, same, 0) - measured) * certain).astype(jnp.bfloat16).astype(jnp.float32)
    spread = jnp.where(select, coef, 0.0).astype(jnp.bfloat16)
    for n, (part, start, w) in enumerate(pieces):
        at = pl.ds(n * unit, unit)
        back = jnp.dot(spread, part[:, pl.ds(start, w)], preferred_element_type=jnp.float32).astype(jnp.bfloat16)
        for p in range(owners):
            adjoint[p][:, at] = back[p * capacity : (p + 1) * capacity]
    modeled[...] = spread_by(entry_sums, member, 0)


def placing_kernel(*refs):
    placing, returned, (out, held, sems) = refs[0], refs[1:-3], refs[-3:]
    place = placing[...]
    copies = []
    for n, (start, width) in enumerate(chunks_of(held.shape[1], held.shape[1] // 8)):
        at = pl.ds(start, width)
        rows = jnp.concatenate([r[:, at] for r in returned], axis=0)
        held[:, at] = lax.dot_general(place, rows, (((0,), (0,)), ((), ())), preferred_element_type=jnp.float32)
        copies.append(pltpu.make_async_copy(held.at[:, at], out.at[:, at], sems.at[n]))
        copies[-1].start()
    for copy in copies:
        copy.wait()


def on_device(flux, footprint, foot_slot, wanted, counts, observed, inv_var):
    steps_win, tiles_dev, cells = flux.shape
    owners = lax.axis_size("tile")
    capacity = wanted.shape[3]
    slots = owners * capacity
    own_rows = steps_win * tiles_dev
    soundings, per = foot_slot.shape[1:]
    entries = soundings * per
    half = functools.partial(jax.ShapeDtypeStruct, dtype=jnp.bfloat16)
    params = pltpu.CompilerParams

    table = wanted.reshape(owners, capacity).T
    ahead = passed_along(table, -1, False)
    prints = footprint.reshape(soundings, per, cells)
    unit = cells // 8
    own = flux.reshape(own_rows, cells)
    small = [table, foot_slot.reshape(soundings, per).T, counts.reshape(1, owners), observed, inv_var]
    shapes = [(entries, PARTS[0] * unit), own.shape] + [x.shape for x in small]
    first, own, table, *small = fetched([prints, own] + small, shapes, 0)
    (second,) = fetched([prints], [(entries, PARTS[1] * unit)], PARTS[0] * unit)
    tables = jnp.stack([table, ahead])[None]
    while tables.shape[0] < owners:
        theirs = swapped(tables, tables.shape[0])
        tables = jnp.concatenate([tables, theirs])

    block = half((capacity, cells))
    gathered = pl.pallas_call(
        functools.partial(gather_kernel, owners, capacity),
        in_specs=[VMEM, VMEM],
        out_specs=[VMEM] * (2 * owners + 1),
        out_shape=[block] * (2 * owners) + [half((2 * slots, own_rows))],
        compiler_params=params(vmem_limit_bytes=16 * MIB),
        name="gather",
    )(tables, own)
    later, now, placing = gathered[:owners], gathered[owners:-1], gathered[-1]

    past, arrived = [None] * owners, [None] * owners
    for p in reversed(range(owners)):
        past[p] = passed_along(later[p], 1, True)
    for p in reversed(range(1, owners)):
        arrived[p] = swapped(past[p] + now[p], p)
    arrived = arrived[1:]

    results = pl.pallas_call(
        functools.partial(adjoint_kernel, owners, capacity, per),
        in_specs=[VMEM, VMEM, HBM] + [VMEM] * (5 + owners),
        out_specs=[VMEM] * (1 + owners),
        out_shape=[jax.ShapeDtypeStruct((1, soundings), jnp.float32)] + [block] * owners,
        scratch_shapes=[pltpu.VMEM((entries, PARTS[2] * unit), jnp.bfloat16), pltpu.SemaphoreType.DMA((PARTS[2],))],
        compiler_params=params(vmem_limit_bytes=20 * MIB),
        name="adjoint",
    )(
        first,
        second,
        in_hbm(prints),
        *small,
        past[0],
        now[0],
        *arrived,
    )
    modeled, adjoint = results[0], results[1:]

    returned, incoming = [adjoint[0]] + [None] * (owners - 1), [None] * owners
    for p in reversed(range(1, owners)):
        returned[p] = swapped(adjoint[p], p)
    for p in range(owners):
        incoming[p] = passed_along(returned[p], -1, True)

    grad = pl.pallas_call(
        placing_kernel,
        in_specs=[VMEM] * (1 + 2 * owners),
        out_specs=HBM,
        out_shape=jax.ShapeDtypeStruct((own_rows, cells), jnp.float32),
        scratch_shapes=[pltpu.VMEM((own_rows, cells), jnp.float32), pltpu.SemaphoreType.DMA((8,))],
        compiler_params=params(vmem_limit_bytes=20 * MIB),
        name="placing",
    )(placing, *incoming, *returned)
    return (modeled, grad.reshape(steps_win, tiles_dev, cells))


def solution(mesh):
    placed = (
        P(("member", "tm"), "tile", None),
        P("tm", "tile", None, None),
        P("tm", "tile", None),
        P("tm", "tile", None, None),
        P("tm", "tile", None),
        P("tm", "tile"),
        P("tm", "tile"),
    )

    return jax.shard_map(
        on_device,
        mesh=mesh,
        in_specs=placed,
        out_specs=(P(("member", "tm"), "tile"), P(("member", "tm"), "tile", None)),
        check_vma=False,
    )
```

time: 49.5 us -> 45.3 us (0.915)
  waiting for transfers between devices: 16.5 us -> 13.7 us
  Pallas kernels: 15.3 us -> 13.5 us
  starting transfers between devices: 15.5 us -> 17 us
  local copies, waits for them, and re-layouts: 0.72 us -> 0 us
    ppermute x5 -> x9, waiting for transfers between devices: 12.7 us -> 9.91 us  [passed_along(): lax.ppermute(value, 'tm', [(source, (source + steps) % count) for source...]
    pallas_call x3 -> x2, Pallas kernels: 6.11 us -> 4.08 us  [fetched(): pl.pallas_call(functools.partial(fetch_kernel, len(sources), start), in_s...]
    ppermute x5 -> x9, starting transfers between devices: 10.6 us -> 11.4 us  [passed_along(): lax.ppermute(value, 'tm', [(source, (source + steps) % count) for source...]
    ppermute x8, starting transfers between devices: 4.87 us -> 5.6 us  [swapped(): lax.ppermute(value, 'tile', [(j, j ^ mask) for j in range(lax.axis_size('...]
    pad x1 -> x0, local copies, waits for them, and re-layouts: 0.72 us -> none  [on_device(): jnp.pad(table[None, None], ((0, 0), (0, 1), (0, 0), (0, 0)))]
  transfers between devices with their start and end apart: 13 -> 17, of which waited for: 9 -> 11; matrix products, arithmetic and copies ran while one was open for 3% -> 0% of each run, Pallas kernels for 12% -> 9%
where the time goes in v1:
time: 45.3 us; the launch traced here: 45.2 us
  starting transfers between devices  17 us (38%)
  waiting for transfers between devices  13.7 us (30%)
  Pallas kernels  13.5 us (30%)
  between operations  0.74 us (2%)
    ppermute x9, starting transfers between devices, passed_along(): lax.ppermute(value, 'tm', [(source, (source + steps) % count) for source...  11.4 us
    ppermute x9, waiting for transfers between devices, passed_along(): lax.ppermute(value, 'tm', [(source, (source + steps) % count) for source...  9.91 us
    pallas_call x1, Pallas kernels, on_device(): pl.pallas_call(functools.partial(adjoint_kernel, owners, capacity, per),...  6.58 us
    ppermute x8, starting transfers between devices, swapped(): lax.ppermute(value, 'tile', [(j, j ^ mask) for j in range(lax.axis_size('...  5.6 us
    pallas_call x2, Pallas kernels, fetched(): pl.pallas_call(functools.partial(fetch_kernel, len(sources), start), in_s...  4.08 us
    ppermute x8, waiting for transfers between devices, swapped(): lax.ppermute(value, 'tile', [(j, j ^ mask) for j in range(lax.axis_size('...  3.79 us
    pallas_call x1, Pallas kernels, on_device(): pl.pallas_call(placing_kernel, in_specs=[VMEM] * (1 + 2 * owners), out_sp...  2.33 us
  transfers between devices with their start and end apart: 17, of which 11 were waited for; matrix products, arithmetic and copies ran while one was open for 0% of the time, Pallas kernels for 9%

profile of v1, /device:TPU:0, one launch (start us, length us, event | category | flops | bytes accessed | tf_op | source)
XLA Modules:
  0.0 45.2 jit_solution(16679701753442420759)
XLA Ops:
  0.6 1.3 %collective-permute-start = (s32[2,4]{1,0:T(2,128)}, s32[2,4]{1,0:T(2,128)S(1)}, u32[]{:S(2)}, u32[]{:S(2)}) collective-permute-start(s32[2,4]{1,0:T(2,128)} %bitcast.21), channel_id=1, source_target_pairs={{4,0},{8,4},{12,8},{5,1},{9,5},{13,9},{6,2},{10,6},{14,10},{7,3},{... | collective-permute-start | bytes 104 | tf_op jit(solution)/shard_map/ppermute | solution.py:20
  1.9 2.1 %shard_map.86 = (bf16[256,2048]{1,0:T(8,128)(2,1)S(1)}, bf16[64,16384]{1,0:T(8,128)(2,1)S(1)}, s32[2,4]{1,0:T(2,128)S(1)}, s32[4,64]{1,0:T(4,128)S(1)}, s32[1,4]...) custom-call(bf16[64,4,16384]{2,1,0:T(4,128)(2,1)} %bitcast.15, bf16[64,16384]{1,0:T(8,128)(2,1)} %bitcast.19, ...), custom_call_target="tpu_custom_call" | custom-call | tf_op jit(solution)/shard_map/pallas_call | solution.py:53
  4.1 3.3 %collective-permute-done = s32[2,4]{1,0:T(2,128)S(1)} collective-permute-done((s32[2,4]{1,0:T(2,128)}, s32[2,4]{1,0:T(2,128)S(1)}, u32[]{:S(2)}, u32[]{:S(2)}) %collective-permute-start) | collective-permute-done | bytes 64 | tf_op jit(solution)/shard_map/ppermute | solution.py:20
  7.4 0.0 collective-permute-start.1
  7.4 1.2 %collective-permute-done.1 = s32[1,2,2,4]{3,2,1,0:T(2,128)S(1)} collective-permute-done((s32[1,2,2,4]{3,2,1,0:T(2,128)S(1)}, s32[1,2,2,4]{3,2,1,0:T(2,128)S(1)}, u32[]{:S(2)}, u32[]{:S(2)}) %collective-permute-start.1) | collective-permute-done | bytes 96 | tf_op jit(solution)/shard_map/ppermute | solution.py:24
  8.5 2.0 %collective-permute-start.2 = (s32[2,2,2,4]{3,2,1,0:T(2,128)S(1)}, s32[2,2,2,4]{3,2,1,0:T(2,128)S(1)}, u32[]{:S(2)}, u32[]{:S(2)}) collective-permute-start(s32[2,2,2,4]{3,2,1,0:T(2,128)S(1)} %pad_add_fusion.1), channel_id=1, source_target_pairs={{0,2},{1,3},{2,0},{3,1},{4,6},{5,7},{6,4},{7,5},{8,10},{9,11},{10,... | collective-permute-start | bytes 392 | tf_op jit(solution)/shard_map/ppermute | solution.py:24
  10.5 1.6 %collective-permute-done.2 = s32[2,2,2,4]{3,2,1,0:T(2,128)S(1)} collective-permute-done((s32[2,2,2,4]{3,2,1,0:T(2,128)S(1)}, s32[2,2,2,4]{3,2,1,0:T(2,128)S(1)}, u32[]{:S(2)}, u32[]{:S(2)}) %collective-permute-start.2) | collective-permute-done | bytes 160 | tf_op jit(solution)/shard_map/ppermute | solution.py:24
  12.1 0.5 %gather.1 = (bf16[2,16384]{1,0:T(2,128)(2,1)S(1)}, bf16[2,16384]{1,0:T(2,128)(2,1)S(1)}, bf16[2,16384]{1,0:T(2,128)(2,1)S(1)}, bf16[2,16384]{1,0:T(2,128)(2,1)S(...) custom-call(s32[4,2,2,4]{3,2,1,0:T(2,128)S(1)} %pad_add_fusion.refs_, ...), custom_call_target="tpu_custom_call" | custom-call | tf_op jit(solution)/shard_map/gather/pallas_call | solution.py:192
  12.6 2.1 %collective-permute-start.8 = (bf16[2,16384]{1,0:T(2,128)(2,1)S(1)}, bf16[2,16384]{1,0:T(2,128)(2,1)S(1)}, u32[]{:S(2)}, u32[]{:S(2)}) collective-permute-start(bf16[2,16384]{1,0:T(2,128)(2,1)S(1)} %get-tuple-element.36), channel_id=1, source_target_pairs={{0,4},{4,8},{8,12},{12,0},{1,5},{5,9},{9,13},{13,1},{2,6},{6,10},{... | collective-permute-start | bytes 196616 | tf_op jit(solution)/shard_map/ppermute | solution.py:20
  14.7 1.6 %collective-permute-start.6 = (bf16[2,16384]{1,0:T(2,128)(2,1)S(1)}, bf16[2,16384]{1,0:T(2,128)(2,1)S(1)}, u32[]{:S(2)}, u32[]{:S(2)}) collective-permute-start(bf16[2,16384]{1,0:T(2,128)(2,1)S(1)} %get-tuple-element.34), channel_id=1, source_target_pairs={{0,4},{4,8},{8,12},{12,0},{1,5},{5,9},{9,13},{13,1},{2,6},{6,10},{... | collective-permute-start | bytes 196616 | tf_op jit(solution)/shard_map/ppermute | solution.py:20
  16.3 0.5 %collective-permute-start.4 = (bf16[2,16384]{1,0:T(2,128)(2,1)S(1)}, bf16[2,16384]{1,0:T(2,128)(2,1)S(1)}, u32[]{:S(2)}, u32[]{:S(2)}) collective-permute-start(bf16[2,16384]{1,0:T(2,128)(2,1)S(1)} %get-tuple-element.32), channel_id=1, source_target_pairs={{0,4},{4,8},{8,12},{12,0},{1,5},{5,9},{9,13},{13,1},{2,6},{6,10},{... | collective-permute-start | bytes 196616 | tf_op jit(solution)/shard_map/ppermute | solution.py:20
  16.7 0.9 %collective-permute-start.3 = (bf16[2,16384]{1,0:T(2,128)(2,1)S(1)}, bf16[2,16384]{1,0:T(2,128)(2,1)S(1)}, u32[]{:S(2)}, u32[]{:S(2)}) collective-permute-start(bf16[2,16384]{1,0:T(2,128)(2,1)S(1)} %get-tuple-element.30), channel_id=1, source_target_pairs={{0,4},{4,8},{8,12},{12,0},{1,5},{5,9},{9,13},{13,1},{2,6},{6,10},{... | collective-permute-start | bytes 196616 | tf_op jit(solution)/shard_map/ppermute | solution.py:20
  17.6 1.7 %collective-permute-done.8 = bf16[2,16384]{1,0:T(2,128)(2,1)S(1)} collective-permute-done((bf16[2,16384]{1,0:T(2,128)(2,1)S(1)}, bf16[2,16384]{1,0:T(2,128)(2,1)S(1)}, u32[]{:S(2)}, u32[]{:S(2)}) %collective-permute-start.8) | collective-permute-done | bytes 65568 | tf_op jit(solution)/shard_map/ppermute | solution.py:20
  19.3 0.1 add.11
  19.4 0.1 collective-permute-start.9
  19.5 1.8 %collective-permute-done.6 = bf16[2,16384]{1,0:T(2,128)(2,1)S(1)} collective-permute-done((bf16[2,16384]{1,0:T(2,128)(2,1)S(1)}, bf16[2,16384]{1,0:T(2,128)(2,1)S(1)}, u32[]{:S(2)}, u32[]{:S(2)}) %collective-permute-start.6) | collective-permute-done | bytes 65568 | tf_op jit(solution)/shard_map/ppermute | solution.py:20
  21.3 0.1 add.10
  21.4 1.6 %collective-permute-start.7 = (bf16[2,16384]{1,0:T(2,128)(2,1)S(1)}, bf16[2,16384]{1,0:T(2,128)(2,1)S(1)}, u32[]{:S(2)}, u32[]{:S(2)}) collective-permute-start(bf16[2,16384]{1,0:T(2,128)(2,1)S(1)} %add.10), channel_id=1, source_target_pairs={{0,2},{1,3},{2,0},{3,1},{4,6},{5,7},{6,4},{7,5},{8,10},{9,11},{10,... | collective-permute-start | bytes 196616 | tf_op jit(solution)/shard_map/ppermute | solution.py:24
  23.0 0.0 collective-permute-done.4
  23.0 0.1 add.9
  23.1 0.1 collective-permute-start.5
  23.2 2.0 %shard_map.87.refs_1_ = bf16[256,6144]{1,0:T(8,128)(2,1)S(1)} custom-call(bf16[64,4,16384]{2,1,0:T(4,128)(2,1)} %bitcast.16), custom_call_target="tpu_custom_call" | custom-call | tf_op jit(solution)/shard_map/pallas_call | solution.py:53
  25.1 0.0 collective-permute-done.3.refs_7_
  25.1 0.0 collective-permute-done.9.refs_11_
  25.1 0.6 %collective-permute-done.7.refs_10_ = bf16[2,16384]{1,0:T(2,128)(2,1)S(1)} collective-permute-done((bf16[2,16384]{1,0:T(2,128)(2,1)S(1)}, bf16[2,16384]{1,0:T(2,128)(2,1)S(1)}, u32[]{:S(2)}, u32[]{:S(2)}) %collective-permute-start.7) | collective-permute-done | bytes 65568 | tf_op jit(solution)/shard_map/ppermute | solution.py:24
  25.7 0.0 collective-permute-done.5.refs_9_
  25.7 6.6 %adjoint.1 = (f32[1,64]{1,0:T(1,128)}, bf16[2,16384]{1,0:T(2,128)(2,1)S(1)}, bf16[2,16384]{1,0:T(2,128)(2,1)S(1)}, bf16[2,16384]{1,0:T(2,128)(2,1)S(1)}, bf16[2,16384]{1,0:T(2,128)(2,1)S(1)}) custom-call(bf16[256,2048]{1,0:T(8,128)(2,1)S(1)} %get-tuple-element.23.refs_0_, bf16[256,6144]{1,0:T(8,128)(2,1)S(1)} %shard_map.87.refs_1_, ...), custom_call_target="tpu_custom_call" | custom-call | tf_op jit(solution)/shard_map/adjoint/pallas_call | solution.py:209
  32.3 0.1 collective-permute-start.11
  32.4 1.6 %collective-permute-start.13 = (bf16[2,16384]{1,0:T(2,128)(2,1)S(1)}, bf16[2,16384]{1,0:T(2,128)(2,1)S(1)}, u32[]{:S(2)}, u32[]{:S(2)}) collective-permute-start(bf16[2,16384]{1,0:T(2,128)(2,1)S(1)} %get-tuple-element.42), channel_id=1, source_target_pairs={{0,2},{1,3},{2,0},{3,1},{4,6},{5,7},{6,4},{7,5},{8,10},{9,11},{10,... | collective-permute-start | bytes 196616 | tf_op jit(solution)/shard_map/ppermute | solution.py:24
  34.0 0.3 collective-permute-start.15
  34.3 0.8 %collective-permute-start.10 = (bf16[2,16384]{1,0:T(2,128)(2,1)S(1)}, bf16[2,16384]{1,0:T(2,128)(2,1)S(1)}, u32[]{:S(2)}, u32[]{:S(2)}) collective-permute-start(bf16[2,16384]{1,0:T(2,128)(2,1)S(1)} %get-tuple-element.40.refs_5_), channel_id=1, source_target_pairs={{0,12},{4,0},{8,4},{12,8},{1,13},{5,1},{9,5},{13,9},{2,14},{6,2},{... | collective-permute-start | bytes 196616 | tf_op jit(solution)/shard_map/ppermute | solution.py:20
  35.0 0.0 collective-permute-done.11.refs_6_
  35.0 1.6 %collective-permute-start.12 = (bf16[2,16384]{1,0:T(2,128)(2,1)S(1)}, bf16[2,16384]{1,0:T(2,128)(2,1)S(1)}, u32[]{:S(2)}, u32[]{:S(2)}) collective-permute-start(bf16[2,16384]{1,0:T(2,128)(2,1)S(1)} %collective-permute-done.11.refs_6_), channel_id=1, source_target_pairs={{0,12},{4,0},{8,4},{12,8},{1,13},{5,1},{9,5},{13,9},{2,14},{6,2},{... | collective-permute-start | bytes 196616 | tf_op jit(solution)/shard_map/ppermute | solution.py:20
  36.6 0.3 collective-permute-done.13.refs_7_
  36.9 1.1 %collective-permute-start.14 = (bf16[2,16384]{1,0:T(2,128)(2,1)S(1)}, bf16[2,16384]{1,0:T(2,128)(2,1)S(1)}, u32[]{:S(2)}, u32[]{:S(2)}) collective-permute-start(bf16[2,16384]{1,0:T(2,128)(2,1)S(1)} %collective-permute-done.13.refs_7_), channel_id=1, source_target_pairs={{0,12},{4,0},{8,4},{12,8},{1,13},{5,1},{9,5},{13,9},{2,14},{6,2},{... | collective-permute-start | bytes 196616 | tf_op jit(solution)/shard_map/ppermute | solution.py:20
  38.0 0.1 collective-permute-done.15.refs_8_
  38.1 1.7 %collective-permute-start.16 = (bf16[2,16384]{1,0:T(2,128)(2,1)S(1)}, bf16[2,16384]{1,0:T(2,128)(2,1)S(1)}, u32[]{:S(2)}, u32[]{:S(2)}) collective-permute-start(bf16[2,16384]{1,0:T(2,128)(2,1)S(1)} %collective-permute-done.15.refs_8_), channel_id=1, source_target_pairs={{0,12},{4,0},{8,4},{12,8},{1,13},{5,1},{9,5},{13,9},{2,14},{6,2},{... | collective-permute-start | bytes 196616 | tf_op jit(solution)/shard_map/ppermute | solution.py:20
  39.8 0.0 collective-permute-done.10.refs_1_
  39.8 0.9 %collective-permute-done.12.refs_2_ = bf16[2,16384]{1,0:T(2,128)(2,1)S(1)} collective-permute-done((bf16[2,16384]{1,0:T(2,128)(2,1)S(1)}, bf16[2,16384]{1,0:T(2,128)(2,1)S(1)}, u32[]{:S(2)}, u32[]{:S(2)}) %collective-permute-start.12) | collective-permute-done | bytes 65568 | tf_op jit(solution)/shard_map/ppermute | solution.py:20
  40.6 1.1 %collective-permute-done.14.refs_3_ = bf16[2,16384]{1,0:T(2,128)(2,1)S(1)} collective-permute-done((bf16[2,16384]{1,0:T(2,128)(2,1)S(1)}, bf16[2,16384]{1,0:T(2,128)(2,1)S(1)}, u32[]{:S(2)}, u32[]{:S(2)}) %collective-permute-start.14) | collective-permute-done | bytes 65568 | tf_op jit(solution)/shard_map/ppermute | solution.py:20
  41.7 1.1 %collective-permute-done.16.refs_4_ = bf16[2,16384]{1,0:T(2,128)(2,1)S(1)} collective-permute-done((bf16[2,16384]{1,0:T(2,128)(2,1)S(1)}, bf16[2,16384]{1,0:T(2,128)(2,1)S(1)}, u32[]{:S(2)}, u32[]{:S(2)}) %collective-permute-start.16) | collective-permute-done | bytes 65568 | tf_op jit(solution)/shard_map/ppermute | solution.py:20
  42.8 2.3 %placing.1 = f32[64,16384]{1,0:T(8,128)} custom-call(bf16[16,64]{1,0:T(8,128)(2,1)S(1)} %get-tuple-element.39.refs_0_, bf16[2,16384]{1,0:T(2,128)(2,1)S(1)} %collective-permute-done.10.refs_1_, bf16[2,16384]{1,0:T(2,128)(2,1)S(1)} %collective-permute-done.12.refs_2_, bf16[2,16384]{1,0:T(2,128)(2,1)S(1)} %collective-permute-done.14.refs_3_, ...), custom_call_target="tpu_custom_call" | custom-call | tf_op jit(solution)/shard_map/placing/pallas_call | solution.py:234
  (3 shorter events, 0.0 us)
Async XLA Ops:
  0.6 6.7 %collective-permute-start = (s32[2,4]{1,0:T(2,128)}, s32[2,4]{1,0:T(2,128)S(1)}, u32[]{:S(2)}, u32[]{:S(2)}) collective-permute-start(s32[2,4]{1,0:T(2,128)} %bitcast.21), channel_id=1, source_target_pairs={{4,0},{8,4},{12,8},{5,1},{9,5},{13,9},{6,2},{10,6},{14,10},{7,3},{... | collective-permute-start | bytes 104 | tf_op jit(solution)/shard_map/ppermute | solution.py:20
  7.4 1.2 %collective-permute-start.1 = (s32[1,2,2,4]{3,2,1,0:T(2,128)S(1)}, s32[1,2,2,4]{3,2,1,0:T(2,128)S(1)}, u32[]{:S(2)}, u32[]{:S(2)}) collective-permute-start(s32[1,2,2,4]{3,2,1,0:T(2,128)S(1)} %add_bitcast_fusion), channel_id=1, source_target_pairs={{0,1},{1,0},{2,3},{3,2},{4,5},{5,4},{6,7},{7,6},{8,9},{9,8},{10,11... | collective-permute-start | bytes 200 | tf_op jit(solution)/shard_map/ppermute | solution.py:24
  8.5 3.6 %collective-permute-start.2 = (s32[2,2,2,4]{3,2,1,0:T(2,128)S(1)}, s32[2,2,2,4]{3,2,1,0:T(2,128)S(1)}, u32[]{:S(2)}, u32[]{:S(2)}) collective-permute-start(s32[2,2,2,4]{3,2,1,0:T(2,128)S(1)} %pad_add_fusion.1), channel_id=1, source_target_pairs={{0,2},{1,3},{2,0},{3,1},{4,6},{5,7},{6,4},{7,5},{8,10},{9,11},{10,... | collective-permute-start | bytes 392 | tf_op jit(solution)/shard_map/ppermute | solution.py:24
  12.6 6.7 %collective-permute-start.8 = (bf16[2,16384]{1,0:T(2,128)(2,1)S(1)}, bf16[2,16384]{1,0:T(2,128)(2,1)S(1)}, u32[]{:S(2)}, u32[]{:S(2)}) collective-permute-start(bf16[2,16384]{1,0:T(2,128)(2,1)S(1)} %get-tuple-element.36), channel_id=1, source_target_pairs={{0,4},{4,8},{8,12},{12,0},{1,5},{5,9},{9,13},{13,1},{2,6},{6,10},{... | collective-permute-start | bytes 196616 | tf_op jit(solution)/shard_map/ppermute | solution.py:20
  14.7 6.6 %collective-permute-start.6 = (bf16[2,16384]{1,0:T(2,128)(2,1)S(1)}, bf16[2,16384]{1,0:T(2,128)(2,1)S(1)}, u32[]{:S(2)}, u32[]{:S(2)}) collective-permute-start(bf16[2,16384]{1,0:T(2,128)(2,1)S(1)} %get-tuple-element.34), channel_id=1, source_target_pairs={{0,4},{4,8},{8,12},{12,0},{1,5},{5,9},{9,13},{13,1},{2,6},{6,10},{... | collective-permute-start | bytes 196616 | tf_op jit(solution)/shard_map/ppermute | solution.py:20
  16.3 6.7 %collective-permute-start.4 = (bf16[2,16384]{1,0:T(2,128)(2,1)S(1)}, bf16[2,16384]{1,0:T(2,128)(2,1)S(1)}, u32[]{:S(2)}, u32[]{:S(2)}) collective-permute-start(bf16[2,16384]{1,0:T(2,128)(2,1)S(1)} %get-tuple-element.32), channel_id=1, source_target_pairs={{0,4},{4,8},{8,12},{12,0},{1,5},{5,9},{9,13},{13,1},{2,6},{6,10},{... | collective-permute-start | bytes 196616 | tf_op jit(solution)/shard_map/ppermute | solution.py:20
  16.7 8.4 %collective-permute-start.3 = (bf16[2,16384]{1,0:T(2,128)(2,1)S(1)}, bf16[2,16384]{1,0:T(2,128)(2,1)S(1)}, u32[]{:S(2)}, u32[]{:S(2)}) collective-permute-start(bf16[2,16384]{1,0:T(2,128)(2,1)S(1)} %get-tuple-element.30), channel_id=1, source_target_pairs={{0,4},{4,8},{8,12},{12,0},{1,5},{5,9},{9,13},{13,1},{2,6},{6,10},{... | collective-permute-start | bytes 196616 | tf_op jit(solution)/shard_map/ppermute | solution.py:20
  19.4 5.7 %collective-permute-start.9 = (bf16[2,16384]{1,0:T(2,128)(2,1)S(1)}, bf16[2,16384]{1,0:T(2,128)(2,1)S(1)}, u32[]{:S(2)}, u32[]{:S(2)}) collective-permute-start(bf16[2,16384]{1,0:T(2,128)(2,1)S(1)} %add.11), channel_id=1, source_target_pairs={{0,3},{1,2},{2,1},{3,0},{4,7},{5,6},{6,5},{7,4},{8,11},{9,10},{10,... | collective-permute-start | bytes 196616 | tf_op jit(solution)/shard_map/ppermute | solution.py:24
  21.4 4.3 %collective-permute-start.7 = (bf16[2,16384]{1,0:T(2,128)(2,1)S(1)}, bf16[2,16384]{1,0:T(2,128)(2,1)S(1)}, u32[]{:S(2)}, u32[]{:S(2)}) collective-permute-start(bf16[2,16384]{1,0:T(2,128)(2,1)S(1)} %add.10), channel_id=1, source_target_pairs={{0,2},{1,3},{2,0},{3,1},{4,6},{5,7},{6,4},{7,5},{8,10},{9,11},{10,... | collective-permute-start | bytes 196616 | tf_op jit(solution)/shard_map/ppermute | solution.py:24
  23.1 2.7 %collective-permute-start.5 = (bf16[2,16384]{1,0:T(2,128)(2,1)S(1)}, bf16[2,16384]{1,0:T(2,128)(2,1)S(1)}, u32[]{:S(2)}, u32[]{:S(2)}) collective-permute-start(bf16[2,16384]{1,0:T(2,128)(2,1)S(1)} %add.9), channel_id=1, source_target_pairs={{0,1},{1,0},{2,3},{3,2},{4,5},{5,4},{6,7},{7,6},{8,9},{9,8},{10,11... | collective-permute-start | bytes 196616 | tf_op jit(solution)/shard_map/ppermute | solution.py:24
  32.3 2.7 %collective-permute-start.11 = (bf16[2,16384]{1,0:T(2,128)(2,1)S(1)}, bf16[2,16384]{1,0:T(2,128)(2,1)S(1)}, u32[]{:S(2)}, u32[]{:S(2)}) collective-permute-start(bf16[2,16384]{1,0:T(2,128)(2,1)S(1)} %get-tuple-element.41), channel_id=1, source_target_pairs={{0,1},{1,0},{2,3},{3,2},{4,5},{5,4},{6,7},{7,6},{8,9},{9,8},{10,11... | collective-permute-start | bytes 196616 | tf_op jit(solution)/shard_map/ppermute | solution.py:24
  32.4 4.5 %collective-permute-start.13 = (bf16[2,16384]{1,0:T(2,128)(2,1)S(1)}, bf16[2,16384]{1,0:T(2,128)(2,1)S(1)}, u32[]{:S(2)}, u32[]{:S(2)}) collective-permute-start(bf16[2,16384]{1,0:T(2,128)(2,1)S(1)} %get-tuple-element.42), channel_id=1, source_target_pairs={{0,2},{1,3},{2,0},{3,1},{4,6},{5,7},{6,4},{7,5},{8,10},{9,11},{10,... | collective-permute-start | bytes 196616 | tf_op jit(solution)/shard_map/ppermute | solution.py:24
  34.0 4.1 %collective-permute-start.15 = (bf16[2,16384]{1,0:T(2,128)(2,1)S(1)}, bf16[2,16384]{1,0:T(2,128)(2,1)S(1)}, u32[]{:S(2)}, u32[]{:S(2)}) collective-permute-start(bf16[2,16384]{1,0:T(2,128)(2,1)S(1)} %get-tuple-element.43), channel_id=1, source_target_pairs={{0,3},{1,2},{2,1},{3,0},{4,7},{5,6},{6,5},{7,4},{8,11},{9,10},{10,... | collective-permute-start | bytes 196616 | tf_op jit(solution)/shard_map/ppermute | solution.py:24
  34.3 5.5 %collective-permute-start.10 = (bf16[2,16384]{1,0:T(2,128)(2,1)S(1)}, bf16[2,16384]{1,0:T(2,128)(2,1)S(1)}, u32[]{:S(2)}, u32[]{:S(2)}) collective-permute-start(bf16[2,16384]{1,0:T(2,128)(2,1)S(1)} %get-tuple-element.40.refs_5_), channel_id=1, source_target_pairs={{0,12},{4,0},{8,4},{12,8},{1,13},{5,1},{9,5},{13,9},{2,14},{6,2},{... | collective-permute-start | bytes 196616 | tf_op jit(solution)/shard_map/ppermute | solution.py:20
  35.0 5.6 %collective-permute-start.12 = (bf16[2,16384]{1,0:T(2,128)(2,1)S(1)}, bf16[2,16384]{1,0:T(2,128)(2,1)S(1)}, u32[]{:S(2)}, u32[]{:S(2)}) collective-permute-start(bf16[2,16384]{1,0:T(2,128)(2,1)S(1)} %collective-permute-done.11.refs_6_), channel_id=1, source_target_pairs={{0,12},{4,0},{8,4},{12,8},{1,13},{5,1},{9,5},{13,9},{2,14},{6,2},{... | collective-permute-start | bytes 196616 | tf_op jit(solution)/shard_map/ppermute | solution.py:20
  36.9 4.8 %collective-permute-start.14 = (bf16[2,16384]{1,0:T(2,128)(2,1)S(1)}, bf16[2,16384]{1,0:T(2,128)(2,1)S(1)}, u32[]{:S(2)}, u32[]{:S(2)}) collective-permute-start(bf16[2,16384]{1,0:T(2,128)(2,1)S(1)} %collective-permute-done.13.refs_7_), channel_id=1, source_target_pairs={{0,12},{4,0},{8,4},{12,8},{1,13},{5,1},{9,5},{13,9},{2,14},{6,2},{... | collective-permute-start | bytes 196616 | tf_op jit(solution)/shard_map/ppermute | solution.py:20
  38.1 4.8 %collective-permute-start.16 = (bf16[2,16384]{1,0:T(2,128)(2,1)S(1)}, bf16[2,16384]{1,0:T(2,128)(2,1)S(1)}, u32[]{:S(2)}, u32[]{:S(2)}) collective-permute-start(bf16[2,16384]{1,0:T(2,128)(2,1)S(1)} %collective-permute-done.15.refs_8_), channel_id=1, source_target_pairs={{0,12},{4,0},{8,4},{12,8},{1,13},{5,1},{9,5},{13,9},{2,14},{6,2},{... | collective-permute-start | bytes 196616 | tf_op jit(solution)/shard_map/ppermute | solution.py:20
